TPU v7x, 32 devices: a whole 2x2x4 slice. The times are simulated.
32 devices in a mesh: gx: 2 (over core), gy: 4 (over y, x), gz: 4 (over z).
Axes of the slice: x: 2, y: 2, z: 4, core: 2. Of those that a mesh axis runs over, the one named last changes fastest.
Arguments:
- features: bfloat16 [4096, 512], P(('gx', 'gy', 'gz')), may hold values from -6 to 6
- halo_index: int32 [3072], P(('gx', 'gy', 'gz')), may hold values from 0 to 127
- edge_src: int32 [128, 384], P(('gx', 'gy', 'gz')), may hold values from 0 to 2623
- edge_dst: int32 [128, 384], P(('gx', 'gy', 'gz')), may hold values from 0 to 127
- edge_count: int32 [128], P(('gx', 'gy', 'gz')), may hold values from 48 to 384, as said below
- edge_basis: bfloat16 [49152, 128], P(('gx', 'gy', 'gz')), may hold values from -6 to 6
- w_edge_in: bfloat16 [4, 1152, 1024], P('gz'), may hold values from -0.1875 to 0.1875
- w_edge_out: bfloat16 [4, 1024, 512], P('gz'), may hold values from -0.1875 to 0.1875
- w_update: bfloat16 [512, 512], replicated, may hold values from -0.25 to 0.25
Outputs:
- new_features: bfloat16 [4096, 512], P(('gx', 'gy', 'gz'))
- halo_next: bfloat16 [832, 96, 512], P(('gx', 'gy', 'gz'))
Inputs may be any that keep to these rules, and one draw needn't show every extreme that they name: The first edge_count slots of a domain's 384 slots for a species pair are live; in every draw some species pair has all 384 slots live in every domain of one gz group.
All inputs are finite; a program needn't handle non-finite values.
Results may differ from a plain program's by a relative error of at most 0.0051.
Values may be sent and summed in bfloat16 or wider, within the bound.
A program may use at most 128 MiB of HBM per device.

v0:
```python
import jax
import jax.numpy as jnp
from jax import lax
from jax.sharding import PartitionSpec as P


def extended(x, sides, width):
    for axis, dim in sides:
        count, length = (lax.axis_size(axis), x.shape[dim])
        up = [(i, (i + 1) % count) for i in range(count)]
        down = [(j, i) for i, j in up]
        last = lax.slice_in_dim(x, length - width, length, axis=dim)
        first = lax.slice_in_dim(x, 0, width, axis=dim)
        before = lax.ppermute(last, axis, up)
        after = lax.ppermute(first, axis, down)
        x = jnp.concatenate([before, x, after], axis=dim)
    return x


def outer_cells(padded):
    flat = padded.reshape(27, padded.shape[3], padded.shape[4])
    return jnp.concatenate([flat[:13], flat[14:]], axis=0)


def shards(
    features,
    halo_index,
    edge_src,
    edge_dst,
    edge_count,
    edge_basis,
    w_edge_in,
    w_edge_out,
    w_update,
):
    model_width = features.shape[1]
    atom_count = features.shape[0]
    group_count = edge_src.shape[0]
    slot_count = edge_src.shape[1]
    first_layer = w_edge_in[0]
    w_source = first_layer[:model_width]
    w_target = first_layer[model_width : 2 * model_width]
    w_radial = first_layer[2 * model_width :]
    w_second = w_edge_out[0]
    boundary = features[halo_index]
    padded = extended(boundary[None, None, None], (("gx", 0), ("gy", 1), ("gz", 2)), 1)
    table_rows = jnp.concatenate([features, outer_cells(padded).reshape(-1, model_width)], axis=0)
    slot_index = lax.broadcasted_iota(jnp.int32, (group_count, slot_count), 1)
    dst_live = jnp.where(slot_index < edge_count[:, None], edge_dst, -1)
    src_rows = table_rows[edge_src]
    basis_rows = edge_basis.reshape(group_count, slot_count, -1)
    owners = lax.all_gather(features, "gz", axis=0, tiled=True)
    source_part = lax.all_to_all(src_rows, "gz", split_axis=0, concat_axis=0, tiled=True)
    radial_part = lax.all_to_all(basis_rows, "gz", split_axis=0, concat_axis=0, tiled=True)
    target_part = lax.all_to_all(dst_live, "gz", split_axis=0, concat_axis=0, tiled=True)
    owner_index = lax.broadcasted_iota(jnp.int32, target_part.shape, 0)
    row_index = owner_index * atom_count + jnp.maximum(target_part, 0)
    pre = jnp.einsum("ock,kh->och", source_part, w_source, preferred_element_type=jnp.float32)
    pre = pre + jnp.einsum(
        "ock,kh->och", owners[row_index], w_target, preferred_element_type=jnp.float32
    )
    pre = pre + jnp.einsum("ock,kh->och", radial_part, w_radial, preferred_element_type=jnp.float32)
    hidden = jax.nn.silu(pre).astype(jnp.bfloat16)
    messages = jnp.einsum(
        "och,hd->ocd", hidden, w_second, preferred_element_type=jnp.float32
    ).astype(jnp.bfloat16)
    atom_iota = lax.broadcasted_iota(jnp.int32, (1, atom_count, 1), 1)
    incidence = (target_part[:, None, :] == atom_iota).astype(jnp.bfloat16)
    partial_value = jnp.einsum(
        "oac,ocd->oad", incidence, messages, preferred_element_type=jnp.float32
    )
    returned = lax.all_to_all(partial_value, "gz", split_axis=0, concat_axis=0, tiled=True)
    summed = jnp.sum(returned, axis=0)
    mean_square = jnp.mean(summed * summed, axis=-1, keepdims=True)
    normed = (summed * lax.rsqrt(mean_square + 1e-05)).astype(jnp.bfloat16)
    update = jnp.dot(normed, w_update, preferred_element_type=jnp.float32)
    new_rows = (features.astype(jnp.float32) + update).astype(jnp.bfloat16)
    boundary_next = new_rows[halo_index]
    padded_next = extended(boundary_next[None, None, None], (("gx", 0), ("gy", 1), ("gz", 2)), 1)
    return (new_rows, outer_cells(padded_next))


def solution(mesh):
    in_specs = (
        P(("gx", "gy", "gz"), None),
        P(("gx", "gy", "gz")),
        P(("gx", "gy", "gz"), None),
        P(("gx", "gy", "gz"), None),
        P(("gx", "gy", "gz")),
        P(("gx", "gy", "gz"), None),
        P("gz", None, None),
        P("gz", None, None),
        P(),
    )
    out_specs = (P(("gx", "gy", "gz"), None), P(("gx", "gy", "gz"), None, None))
    return jax.shard_map(shards, mesh=mesh, in_specs=in_specs, out_specs=out_specs, check_vma=False)
```

profile of v0, /device:TPU:0, one launch (start us, length us, event | category | flops | bytes accessed | tf_op | source)
XLA Modules:
  0.0 244.4 jit_solution(17518737411660622284)
XLA Ops:
  1.4 1.7 gather_fusion
  5.0 3.6 %collective-permute-start.3 = (bf16[3,1,1,96,512]{4,3,2,1,0:T(8,128)(2,1)S(1)}, bf16[3,1,1,96,512]{4,3,2,1,0:T(8,128)(2,1)S(1)}, u32[]{:S(2)}, u32[]{:S(2)}) collective-permute-start(bf16[3,1,1,96,512]{4,3,2,1,0:T(8,128)(2,1)S(1)} %pad_maximum_fusion.7), channel_id=1, source_target_pairs={{4,0},{8,4},{12,8},{0,12},{5,1},{9,5},{13,9},{1,13},{6,2},{10,6},{... | collective-permute-start | bytes 884744 | tf_op jit(solution)/shard_map/ppermute | solution.py:15
  8.7 7.4 %collective-permute-done.3 = bf16[3,1,1,96,512]{4,3,2,1,0:T(8,128)(2,1)S(1)} collective-permute-done((bf16[3,1,1,96,512]{4,3,2,1,0:T(8,128)(2,1)S(1)}, bf16[3,1,1,96,512]{4,3,2,1,0:T(8,128)(2,1)S(1)}, u32[]{:S(2)}, u32[]{:S(2)}) %collective-permute-start.3) | collective-permute-done | bytes 294944 | tf_op jit(solution)/shard_map/ppermute | solution.py:15
  16.1 6.7 %collective-permute-done.2 = bf16[3,1,1,96,512]{4,3,2,1,0:T(8,128)(2,1)S(1)} collective-permute-done((bf16[3,1,1,96,512]{4,3,2,1,0:T(8,128)(2,1)S(1)}, bf16[3,1,1,96,512]{4,3,2,1,0:T(8,128)(2,1)S(1)}, u32[]{:S(2)}, u32[]{:S(2)}) %collective-permute-start.2) | collective-permute-done | bytes 294944 | tf_op jit(solution)/shard_map/ppermute | solution.py:14
  22.9 3.7 %collective-permute-start.5 = (bf16[3,3,1,96,512]{4,3,2,1,0:T(8,128)(2,1)S(1)}, bf16[3,3,1,96,512]{4,3,2,1,0:T(8,128)(2,1)S(1)}, u32[]{:S(2)}, u32[]{:S(2)}) collective-permute-start(bf16[3,3,1,96,512]{4,3,2,1,0:T(8,128)(2,1)S(1)} %pad_maximum_fusion.5), channel_id=1, source_target_pairs={{1,0},{2,1},{3,2},{0,3},{5,4},{6,5},{7,6},{4,7},{9,8},{10,9},{11,1... | collective-permute-start | bytes 2654216 | tf_op jit(solution)/shard_map/ppermute | solution.py:15
  27.2 5.1 %all-to-all-start = ((s32[4,1,384]{2,1,0:T(1,128)}), s32[4,1,384]{2,1,0:T(1,128)S(1)}, u32[]{:S(2)}, u32[]{:S(2)}) async-start(s32[4,1,384]{2,1,0:T(1,128)} %all_to_all.15), calls=%async_computation | async-start | bytes 12288 | tf_op jit(solution)/shard_map/all_to_all | solution.py:55
  32.4 14.2 %collective-permute-done.5 = bf16[3,3,1,96,512]{4,3,2,1,0:T(8,128)(2,1)S(1)} collective-permute-done((bf16[3,3,1,96,512]{4,3,2,1,0:T(8,128)(2,1)S(1)}, bf16[3,3,1,96,512]{4,3,2,1,0:T(8,128)(2,1)S(1)}, u32[]{:S(2)}, u32[]{:S(2)}) %collective-permute-start.5) | collective-permute-done | bytes 884768 | tf_op jit(solution)/shard_map/ppermute | solution.py:15
  46.6 18.6 %collective-permute-done.4 = bf16[3,3,1,96,512]{4,3,2,1,0:T(8,128)(2,1)} collective-permute-done((bf16[3,3,1,96,512]{4,3,2,1,0:T(8,128)(2,1)S(1)}, bf16[3,3,1,96,512]{4,3,2,1,0:T(8,128)(2,1)}, u32[]{:S(2)}, u32[]{:S(2)}) %collective-permute-start.4) | collective-permute-done | bytes 884768 | tf_op jit(solution)/shard_map/ppermute | solution.py:14
  67.7 1.7 pad_maximum_fusion
  69.4 7.6 %gather_fusion.1 = bf16[1536,512]{1,0:T(8,128)(2,1)} fusion(bf16[2624,512]{1,0:T(8,128)(2,1)} %pad_maximum_fusion, s32[2048]{0:T(1024)S(1)} %pad_clamp_fusion.1), kind=kCustom, calls=%fused_computation.1 | custom fusion | bytes 3151872 | tf_op jit(solution)/shard_map/gather | solution.py:50
  77.0 3.6 %all-to-all-start.1 = ((bf16[4,384,512]{2,1,0:T(8,128)(2,1)}), bf16[4,384,512]{2,1,0:T(8,128)(2,1)S(1)}, u32[]{:S(2)}, u32[]{:S(2)}) async-start(bf16[4,384,512]{2,1,0:T(8,128)(2,1)} %bitcast.3), calls=%async_computation.1 | async-start | bytes 3145728 | tf_op jit(solution)/shard_map/all_to_all | solution.py:53
  80.5 46.3 %all_gather.3 = bf16[512,512]{1,0:T(8,128)(2,1)S(1)} all-gather(bf16[128,512]{1,0:T(8,128)(2,1)S(1)} %copy-done.1), channel_id=1, replica_groups=mesh['gx'=2,'gy'=4,'gz'=4] {'gz'}, dimensions={0}, use_global_device_ids=true | all-gather | bytes 655360 | tf_op jit(solution)/shard_map/all_gather | solution.py:52
  127.0 5.4 %gather_fusion.2 = bf16[1536,512]{1,0:T(8,128)(2,1)} fusion(bf16[512,512]{1,0:T(8,128)(2,1)S(1)} %all_gather.3, s32[2048]{0:T(1024)S(1)} %pad_clamp_fusion), kind=kCustom, calls=%fused_computation.2 | custom fusion | bytes 3151872 | tf_op jit(solution)/shard_map/gather | solution.py:60
  132.4 4.6 %all-to-all-start.2 = ((bf16[4,384,128]{2,1,0:T(8,128)(2,1)}), bf16[4,384,128]{2,1,0:T(8,128)(2,1)S(1)}, u32[]{:S(2)}, u32[]{:S(2)}) async-start(bf16[4,384,128]{2,1,0:T(8,128)(2,1)} %bitcast.51), calls=%async_computation.2 | async-start | bytes 786432 | tf_op jit(solution)/shard_map/all_to_all | solution.py:54
  137.0 6.2 %fusion.6 = f32[4,384,1024]{2,1,0:T(8,128)} fusion(bf16[4,384,512]{2,1,0:T(8,128)(2,1)} %bitcast.40, bf16[1,1152,1024]{2,1,0:T(8,128)(2,1)} %param.15), kind=kOutput, calls=%fused_computation.16 | convolution fusion | flops 1610612736 | bytes 8912896 | tf_op jit(solution)/shard_map/ock,kh->och/dot_general | solution.py:59
  143.2 5.6 %fusion.8 = f32[4,384,1024]{2,1,0:T(8,128)} fusion(bf16[4,384,512]{2,1,0:T(8,128)(2,1)S(1)} %all-to-all-done.1, bf16[1,1152,1024]{2,1,0:T(8,128)(2,1)} %param.15), kind=kOutput, calls=%fused_computation.18 | convolution fusion | flops 1610612736 | bytes 8912896 | tf_op jit(solution)/shard_map/ock,kh->och/dot_general | solution.py:58
  148.8 8.0 %fusion.3 = bf16[4,384,512]{2,1,0:T(8,128)(2,1)S(1)} fusion(f32[4,384,1024]{2,1,0:T(8,128)} %fusion.8, f32[4,384,1024]{2,1,0:T(8,128)} %fusion.6, bf16[4,384,128]{2,1,0:T(8,128)(2,1)S(1)} %all-to-all-done.2, bf16[1,1024,512]{2,1,0:T(8,128)(2,1)S(1)} %copy-done, bf16[1,1152,1024]{2,1,0:T(8,128)(2,1)} %param.15), kind=kOutput, calls=%fused_computation.12 | convolution fusion | flops 2025062400 | bytes 15859712 | tf_op jit(solution)/shard_map/och,hd->ocd/dot_general | solution.py:64
  157.3 26.3 %all_to_all.24 = f32[4,128,512]{2,1,0:T(8,128)S(1)} all-to-all(f32[4,128,512]{2,1,0:T(8,128)S(1)} %fusion.12), channel_id=1, replica_groups=mesh['gx'=2,'gy'=4,'gz'=4] {'gz'}, dimensions={0} | all-to-all | bytes 2097152 | tf_op jit(solution)/shard_map/all_to_all | solution.py:72
  186.4 1.5 collective-permute-start.9
  188.5 7.9 %collective-permute-done.9 = bf16[3,1,1,96,512]{4,3,2,1,0:T(8,128)(2,1)S(1)} collective-permute-done((bf16[3,1,1,96,512]{4,3,2,1,0:T(8,128)(2,1)S(1)}, bf16[3,1,1,96,512]{4,3,2,1,0:T(8,128)(2,1)S(1)}, u32[]{:S(2)}, u32[]{:S(2)}) %collective-permute-start.9) | collective-permute-done | bytes 294944 | tf_op jit(solution)/shard_map/ppermute | solution.py:15
  196.3 5.7 %collective-permute-done.8 = bf16[3,1,1,96,512]{4,3,2,1,0:T(8,128)(2,1)S(1)} collective-permute-done((bf16[3,1,1,96,512]{4,3,2,1,0:T(8,128)(2,1)S(1)}, bf16[3,1,1,96,512]{4,3,2,1,0:T(8,128)(2,1)S(1)}, u32[]{:S(2)}, u32[]{:S(2)}) %collective-permute-start.8) | collective-permute-done | bytes 294944 | tf_op jit(solution)/shard_map/ppermute | solution.py:14
  202.1 1.5 collective-permute-start.11
  204.2 38.0 %collective-permute-done.11 = bf16[3,3,1,96,512]{4,3,2,1,0:T(8,128)(2,1)S(1)} collective-permute-done((bf16[3,3,1,96,512]{4,3,2,1,0:T(8,128)(2,1)S(1)}, bf16[3,3,1,96,512]{4,3,2,1,0:T(8,128)(2,1)S(1)}, u32[]{:S(2)}, u32[]{:S(2)}) %collective-permute-start.11) | collective-permute-done | bytes 884768 | tf_op jit(solution)/shard_map/ppermute | solution.py:15
  242.7 1.7 pad_maximum_fusion.4
  (61 shorter events, 11.1 us)
Async XLA Ops:
  0.6 148.2 %copy-start = (bf16[1,1024,512]{2,1,0:T(8,128)(2,1)S(1)}, bf16[1,1024,512]{2,1,0:T(8,128)(2,1)}, u32[]{:S(2)}) copy-start(bf16[1,1024,512]{2,1,0:T(8,128)(2,1)} %param.16) | copy-start | bytes 3145732
  0.6 25.9 %copy-start.8 = (s32[4]{0:T(128)S(1)}, s32[4]{0:T(128)}, u32[]{:S(2)}) copy-start(s32[4]{0:T(128)} %param.13) | copy-start | bytes 52
  0.7 25.9 %copy-start.6 = (s32[4,384]{1,0:T(4,128)S(1)}, s32[4,384]{1,0:T(4,128)}, u32[]{:S(2)}) copy-start(s32[4,384]{1,0:T(4,128)} %param.12) | copy-start | bytes 18436
  0.7 31.7 %copy-start.7 = (s32[4,384]{1,0:T(4,128)S(1)}, s32[4,384]{1,0:T(4,128)}, u32[]{:S(2)}) copy-start(s32[4,384]{1,0:T(4,128)} %param.11) | copy-start | bytes 18436
  3.1 1.5 collective-permute-start.1
  3.7 1.3 collective-permute-start
  4.6 21.9 %copy-start.3 = (bf16[1,1,1,96,512]{4,3,2,1,0:T(8,128)(2,1)}, bf16[1,1,1,96,512]{4,3,2,1,0:T(8,128)(2,1)S(1)}, u32[]{:S(2)}) copy-start(bf16[1,1,1,96,512]{4,3,2,1,0:T(8,128)(2,1)S(1)} %collective-permute-done.1) | copy-start | bytes 294916
  5.0 21.6 %copy-start.4 = (bf16[1,1,1,96,512]{4,3,2,1,0:T(8,128)(2,1)}, bf16[1,1,1,96,512]{4,3,2,1,0:T(8,128)(2,1)S(1)}, u32[]{:S(2)}) copy-start(bf16[1,1,1,96,512]{4,3,2,1,0:T(8,128)(2,1)S(1)} %collective-permute-done) | copy-start | bytes 294916
  5.0 11.0 %collective-permute-start.3 = (bf16[3,1,1,96,512]{4,3,2,1,0:T(8,128)(2,1)S(1)}, bf16[3,1,1,96,512]{4,3,2,1,0:T(8,128)(2,1)S(1)}, u32[]{:S(2)}, u32[]{:S(2)}) collective-permute-start(bf16[3,1,1,96,512]{4,3,2,1,0:T(8,128)(2,1)S(1)} %pad_maximum_fusion.7), channel_id=1, source_target_pairs={{4,0},{8,4},{12,8},{0,12},{5,1},{9,5},{13,9},{1,13},{6,2},{10,6},{... | collective-permute-start | bytes 884744 | tf_op jit(solution)/shard_map/ppermute | solution.py:15
  8.7 14.1 %collective-permute-start.2 = (bf16[3,1,1,96,512]{4,3,2,1,0:T(8,128)(2,1)S(1)}, bf16[3,1,1,96,512]{4,3,2,1,0:T(8,128)(2,1)S(1)}, u32[]{:S(2)}, u32[]{:S(2)}) collective-permute-start(bf16[3,1,1,96,512]{4,3,2,1,0:T(8,128)(2,1)S(1)} %pad_maximum_fusion.7), channel_id=1, source_target_pairs={{0,4},{4,8},{8,12},{12,0},{1,5},{5,9},{9,13},{13,1},{2,6},{6,10},{... | collective-permute-start | bytes 884744 | tf_op jit(solution)/shard_map/ppermute | solution.py:14
  22.9 23.7 %collective-permute-start.5 = (bf16[3,3,1,96,512]{4,3,2,1,0:T(8,128)(2,1)S(1)}, bf16[3,3,1,96,512]{4,3,2,1,0:T(8,128)(2,1)S(1)}, u32[]{:S(2)}, u32[]{:S(2)}) collective-permute-start(bf16[3,3,1,96,512]{4,3,2,1,0:T(8,128)(2,1)S(1)} %pad_maximum_fusion.5), channel_id=1, source_target_pairs={{1,0},{2,1},{3,2},{0,3},{5,4},{6,5},{7,6},{4,7},{9,8},{10,9},{11,1... | collective-permute-start | bytes 2654216 | tf_op jit(solution)/shard_map/ppermute | solution.py:15
  26.5 38.6 %collective-permute-start.4 = (bf16[3,3,1,96,512]{4,3,2,1,0:T(8,128)(2,1)S(1)}, bf16[3,3,1,96,512]{4,3,2,1,0:T(8,128)(2,1)}, u32[]{:S(2)}, u32[]{:S(2)}) collective-permute-start(bf16[3,3,1,96,512]{4,3,2,1,0:T(8,128)(2,1)S(1)} %pad_maximum_fusion.5), channel_id=1, source_target_pairs={{0,1},{1,2},{2,3},{3,0},{4,5},{5,6},{6,7},{7,4},{8,9},{9,10},{10,1... | collective-permute-start | bytes 2654216 | tf_op jit(solution)/shard_map/ppermute | solution.py:14
  27.2 49.7 %all-to-all-start = ((s32[4,1,384]{2,1,0:T(1,128)}), s32[4,1,384]{2,1,0:T(1,128)S(1)}, u32[]{:S(2)}, u32[]{:S(2)}) async-start(s32[4,1,384]{2,1,0:T(1,128)} %all_to_all.15), calls=%async_computation | async-start | bytes 12288 | tf_op jit(solution)/shard_map/all_to_all | solution.py:55
  66.7 0.9 copy-start.1
  77.0 55.5 %all-to-all-start.1 = ((bf16[4,384,512]{2,1,0:T(8,128)(2,1)}), bf16[4,384,512]{2,1,0:T(8,128)(2,1)S(1)}, u32[]{:S(2)}, u32[]{:S(2)}) async-start(bf16[4,384,512]{2,1,0:T(8,128)(2,1)} %bitcast.3), calls=%async_computation.1 | async-start | bytes 3145728 | tf_op jit(solution)/shard_map/all_to_all | solution.py:53
  132.4 16.4 %all-to-all-start.2 = ((bf16[4,384,128]{2,1,0:T(8,128)(2,1)}), bf16[4,384,128]{2,1,0:T(8,128)(2,1)S(1)}, u32[]{:S(2)}, u32[]{:S(2)}) async-start(bf16[4,384,128]{2,1,0:T(8,128)(2,1)} %bitcast.51), calls=%async_computation.2 | async-start | bytes 786432 | tf_op jit(solution)/shard_map/all_to_all | solution.py:54
  156.8 26.9 %copy-start.5 = (bf16[512,512]{1,0:T(8,128)(2,1)S(1)}, bf16[512,512]{1,0:T(8,128)(2,1)}, u32[]{:S(2)}) copy-start(bf16[512,512]{1,0:T(8,128)(2,1)} %param.17) | copy-start | bytes 1572868
  184.0 58.5 %copy-start.2 = (bf16[128,512]{1,0:T(8,128)(2,1)}, bf16[128,512]{1,0:T(8,128)(2,1)S(1)}, u32[]{:S(2)}) copy-start(bf16[128,512]{1,0:T(8,128)(2,1)S(1)} %fusion.4) | copy-start | bytes 393220
  184.8 1.4 collective-permute-start.7
  184.9 1.4 collective-permute-start.6
  186.4 9.9 %collective-permute-start.9 = (bf16[3,1,1,96,512]{4,3,2,1,0:T(8,128)(2,1)S(1)}, bf16[3,1,1,96,512]{4,3,2,1,0:T(8,128)(2,1)S(1)}, u32[]{:S(2)}, u32[]{:S(2)}) collective-permute-start(bf16[3,1,1,96,512]{4,3,2,1,0:T(8,128)(2,1)S(1)} %pad_maximum_fusion.8), channel_id=1, source_target_pairs={{4,0},{8,4},{12,8},{0,12},{5,1},{9,5},{13,9},{1,13},{6,2},{10,6},{... | collective-permute-start | bytes 884744 | tf_op jit(solution)/shard_map/ppermute | solution.py:15
  187.9 14.1 %collective-permute-start.8 = (bf16[3,1,1,96,512]{4,3,2,1,0:T(8,128)(2,1)S(1)}, bf16[3,1,1,96,512]{4,3,2,1,0:T(8,128)(2,1)S(1)}, u32[]{:S(2)}, u32[]{:S(2)}) collective-permute-start(bf16[3,1,1,96,512]{4,3,2,1,0:T(8,128)(2,1)S(1)} %pad_maximum_fusion.8), channel_id=1, source_target_pairs={{0,4},{4,8},{8,12},{12,0},{1,5},{5,9},{9,13},{13,1},{2,6},{6,10},{... | collective-permute-start | bytes 884744 | tf_op jit(solution)/shard_map/ppermute | solution.py:14
  202.1 40.1 %collective-permute-start.11 = (bf16[3,3,1,96,512]{4,3,2,1,0:T(8,128)(2,1)S(1)}, bf16[3,3,1,96,512]{4,3,2,1,0:T(8,128)(2,1)S(1)}, u32[]{:S(2)}, u32[]{:S(2)}) collective-permute-start(bf16[3,3,1,96,512]{4,3,2,1,0:T(8,128)(2,1)S(1)} %pad_maximum_fusion.6), channel_id=1, source_target_pairs={{1,0},{2,1},{3,2},{0,3},{5,4},{6,5},{7,6},{4,7},{9,8},{10,9},{11,1... | collective-permute-start | bytes 2654216 | tf_op jit(solution)/shard_map/ppermute | solution.py:15
  203.6 38.6 %collective-permute-start.10 = (bf16[3,3,1,96,512]{4,3,2,1,0:T(8,128)(2,1)S(1)}, bf16[3,3,1,96,512]{4,3,2,1,0:T(8,128)(2,1)S(1)}, u32[]{:S(2)}, u32[]{:S(2)}) collective-permute-start(bf16[3,3,1,96,512]{4,3,2,1,0:T(8,128)(2,1)S(1)} %pad_maximum_fusion.6), channel_id=1, source_target_pairs={{0,1},{1,2},{2,3},{3,0},{4,5},{5,6},{6,7},{7,4},{8,9},{9,10},{10,1... | collective-permute-start | bytes 2654216 | tf_op jit(solution)/shard_map/ppermute | solution.py:14
where the time goes:
time: 245 us; the launch traced here: 244 us
  waiting for transfers between devices  101 us (41%)
  blocking collectives  72.6 us (30%)
  starting transfers between devices  25.9 us (11%)
  matrix products  20.5 us (8%)
  local copies, waits for them, and re-layouts  17.2 us (7%)
  other arithmetic  6.8 us (3%)
    ppermute x6, waiting for transfers between devices, extended(): after = lax.ppermute(first, axis, down)  69.1 us
    all_gather x1, blocking collectives, shards(): owners = lax.all_gather(features, 'gz', axis=0, tiled=True)  46.3 us
    ppermute x6, waiting for transfers between devices, extended(): before = lax.ppermute(last, axis, up)  31.4 us
    all_to_all x1, blocking collectives, shards(): lax.all_to_all(partial_value, 'gz', split_axis=0, concat_axis=0, tiled=True)  26.3 us
    ppermute x6, starting transfers between devices, extended(): after = lax.ppermute(first, axis, down)  10.9 us
    dot_general x1, matrix products, shards(): jnp.einsum('och,hd->ocd', hidden, w_second, preferred_element_type=jnp.fl...  7.98 us
    gather x1, local copies, waits for them, and re-layouts, shards(): src_rows = table_rows[edge_src]  7.59 us
    dot_general x1, matrix products, shards(): jnp.einsum('ock,kh->och', owners[row_index], w_target, preferred_element_...  6.17 us
  transfers between devices with their start and end apart: 15, of which 11 were waited for; matrix products, arithmetic and copies ran while one was open for 12% of the time, Pallas kernels for 0%

commit v1 on v0

--- a/solution.py
+++ b/solution.py
@@ -1,7 +1,26 @@
+import functools
 import jax
 import jax.numpy as jnp
 from jax import lax
 from jax.sharding import PartitionSpec as P
+
+
+def _resolve_words(shard_in, bus_axis):
+    many = jax.lax.axis_size(bus_axis)
+    odd = [(h - 1, h) for h in range(1, many)] + [(many - 1, 0)]
+    long_array = shard_in
+    kept_rows = [long_array]
+    for _ in [*range(many - 1)]:
+        long_array = jax.lax.ppermute(long_array, axis_name=bus_axis, perm=odd)
+        kept_rows += [long_array]
+    return jnp.roll(
+        jnp.concatenate([*reversed(kept_rows)], axis=0),
+        shift=(jax.lax.axis_index(bus_axis) + 1) * long_array.shape[0],
+        axis=0,
+    )
+
+
+_report_state = functools.partial(_resolve_words, bus_axis="gz")
 
 
 def extended(x, sides, width):
@@ -49,7 +68,7 @@
     dst_live = jnp.where(slot_index < edge_count[:, None], edge_dst, -1)
     src_rows = table_rows[edge_src]
     basis_rows = edge_basis.reshape(group_count, slot_count, -1)
-    owners = lax.all_gather(features, "gz", axis=0, tiled=True)
+    owners = _report_state(features)
     source_part = lax.all_to_all(src_rows, "gz", split_axis=0, concat_axis=0, tiled=True)
     radial_part = lax.all_to_all(basis_rows, "gz", split_axis=0, concat_axis=0, tiled=True)
     target_part = lax.all_to_all(dst_live, "gz", split_axis=0, concat_axis=0, tiled=True)

time: 245 us -> 246 us (level)
  blocking collectives: 72.6 us -> 25.2 us
  waiting for transfers between devices: 101 us -> 138 us
  starting transfers between devices: 25.9 us -> 37.1 us
    all_gather x1 -> x0, blocking collectives: 46.3 us -> none  [shards(): owners = lax.all_gather(features, 'gz', axis=0, tiled=True)]
    ppermute x0 -> x3, waiting for transfers between devices: none -> 37 us  [_resolve_words(): long_array = jax.lax.ppermute(long_array, axis_name=bus_axis, perm=odd)]
    all_to_all x1, waiting for transfers between devices: 0.01 us -> 32.8 us  [shards(): lax.all_to_all(dst_live, 'gz', split_axis=0, concat_axis=0, tiled=True)]
    ppermute x6, waiting for transfers between devices: 31.4 us -> 12.9 us  [extended(): before = lax.ppermute(last, axis, up)]
    ppermute x6, waiting for transfers between devices: 69.1 us -> 54.9 us  [extended(): after = lax.ppermute(first, axis, down)]
    ppermute x0 -> x3, starting transfers between devices: none -> 11 us  [_resolve_words(): long_array = jax.lax.ppermute(long_array, axis_name=bus_axis, perm=odd)]
  transfers between devices with their start and end apart: 15 -> 18, of which waited for: 11 -> 13; matrix products, arithmetic and copies ran while one was open for 12% -> 7% of each run, Pallas kernels for 0% -> 0%
where the time goes in v1:
time: 246 us; the launch traced here: 245 us
  waiting for transfers between devices  138 us (56%)
  starting transfers between devices  37.1 us (15%)
  blocking collectives  25.2 us (10%)
  matrix products  20.5 us (8%)
  local copies, waits for them, and re-layouts  17.3 us (7%)
  other arithmetic  6.8 us (3%)
    ppermute x6, waiting for transfers between devices, extended(): after = lax.ppermute(first, axis, down)  54.9 us
    ppermute x3, waiting for transfers between devices, _resolve_words(): long_array = jax.lax.ppermute(long_array, axis_name=bus_axis, perm=odd)  37 us
    all_to_all x1, waiting for transfers between devices, shards(): lax.all_to_all(dst_live, 'gz', split_axis=0, concat_axis=0, tiled=True)  32.8 us
    all_to_all x1, blocking collectives, shards(): lax.all_to_all(partial_value, 'gz', split_axis=0, concat_axis=0, tiled=True)  25.2 us
    ppermute x6, waiting for transfers between devices, extended(): before = lax.ppermute(last, axis, up)  12.9 us
    ppermute x3, starting transfers between devices, _resolve_words(): long_array = jax.lax.ppermute(long_array, axis_name=bus_axis, perm=odd)  11 us
    ppermute x6, starting transfers between devices, extended(): after = lax.ppermute(first, axis, down)  10.9 us
    dot_general x1, matrix products, shards(): jnp.einsum('och,hd->ocd', hidden, w_second, preferred_element_type=jnp.fl...  7.98 us
  transfers between devices with their start and end apart: 18, of which 13 were waited for; matrix products, arithmetic and copies ran while one was open for 7% of the time, Pallas kernels for 0%

profile of v1, /device:TPU:0, one launch (start us, length us, event | category | flops | bytes accessed | tf_op | source)
XLA Modules:
  0.0 245.3 jit_solution(9217928876491454360)
XLA Ops:
  1.4 1.7 gather_fusion
  5.0 3.6 %collective-permute-start.3 = (bf16[3,1,1,96,512]{4,3,2,1,0:T(8,128)(2,1)S(1)}, bf16[3,1,1,96,512]{4,3,2,1,0:T(8,128)(2,1)S(1)}, u32[]{:S(2)}, u32[]{:S(2)}) collective-permute-start(bf16[3,1,1,96,512]{4,3,2,1,0:T(8,128)(2,1)S(1)} %pad_maximum_fusion.7), channel_id=1, source_target_pairs={{4,0},{8,4},{12,8},{0,12},{5,1},{9,5},{13,9},{1,13},{6,2},{10,6},{... | collective-permute-start | bytes 884744 | tf_op jit(solution)/shard_map/ppermute | solution.py:34
  8.7 7.4 %collective-permute-done.3 = bf16[3,1,1,96,512]{4,3,2,1,0:T(8,128)(2,1)S(1)} collective-permute-done((bf16[3,1,1,96,512]{4,3,2,1,0:T(8,128)(2,1)S(1)}, bf16[3,1,1,96,512]{4,3,2,1,0:T(8,128)(2,1)S(1)}, u32[]{:S(2)}, u32[]{:S(2)}) %collective-permute-start.3) | collective-permute-done | bytes 294944 | tf_op jit(solution)/shard_map/ppermute | solution.py:34
  16.1 6.7 %collective-permute-done.2 = bf16[3,1,1,96,512]{4,3,2,1,0:T(8,128)(2,1)S(1)} collective-permute-done((bf16[3,1,1,96,512]{4,3,2,1,0:T(8,128)(2,1)S(1)}, bf16[3,1,1,96,512]{4,3,2,1,0:T(8,128)(2,1)S(1)}, u32[]{:S(2)}, u32[]{:S(2)}) %collective-permute-start.2) | collective-permute-done | bytes 294944 | tf_op jit(solution)/shard_map/ppermute | solution.py:33
  22.9 3.7 %collective-permute-start.5 = (bf16[3,3,1,96,512]{4,3,2,1,0:T(8,128)(2,1)S(1)}, bf16[3,3,1,96,512]{4,3,2,1,0:T(8,128)(2,1)S(1)}, u32[]{:S(2)}, u32[]{:S(2)}) collective-permute-start(bf16[3,3,1,96,512]{4,3,2,1,0:T(8,128)(2,1)S(1)} %pad_maximum_fusion.5), channel_id=1, source_target_pairs={{1,0},{2,1},{3,2},{0,3},{5,4},{6,5},{7,6},{4,7},{9,8},{10,9},{11,1... | collective-permute-start | bytes 2654216 | tf_op jit(solution)/shard_map/ppermute | solution.py:34
  27.2 5.1 %all-to-all-start = ((s32[4,1,384]{2,1,0:T(1,128)}), s32[4,1,384]{2,1,0:T(1,128)S(1)}, u32[]{:S(2)}, u32[]{:S(2)}) async-start(s32[4,1,384]{2,1,0:T(1,128)} %all_to_all.15), calls=%async_computation | async-start | bytes 12288 | tf_op jit(solution)/shard_map/all_to_all | solution.py:74
  32.4 32.8 %all-to-all-done = s32[4,1,384]{2,1,0:T(1,128)S(1)} async-done(((s32[4,1,384]{2,1,0:T(1,128)}), s32[4,1,384]{2,1,0:T(1,128)S(1)}, u32[]{:S(2)}, u32[]{:S(2)}) %all-to-all-start) | async-done | bytes 6176 | tf_op jit(solution)/shard_map/all_to_all | solution.py:74
  69.5 7.6 %gather_fusion.1 = bf16[1536,512]{1,0:T(8,128)(2,1)} fusion(bf16[2624,512]{1,0:T(8,128)(2,1)} %pad_maximum_fusion, s32[2048]{0:T(1024)S(1)} %get-tuple-element.7), kind=kCustom, calls=%fused_computation.1 | custom fusion | bytes 3151872 | tf_op jit(solution)/shard_map/gather | solution.py:69
  77.1 4.6 %all-to-all-start.1 = ((bf16[4,384,512]{2,1,0:T(8,128)(2,1)}), bf16[4,384,512]{2,1,0:T(8,128)(2,1)S(1)}, u32[]{:S(2)}, u32[]{:S(2)}) async-start(bf16[4,384,512]{2,1,0:T(8,128)(2,1)} %bitcast.3), calls=%async_computation.1 | async-start | bytes 3145728 | tf_op jit(solution)/shard_map/all_to_all | solution.py:72
  81.7 2.0 collective-permute-start.6
  83.7 28.9 %collective-permute-done.6 = bf16[128,512]{1,0:T(8,128)(2,1)S(1)} collective-permute-done((bf16[128,512]{1,0:T(8,128)(2,1)S(1)}, bf16[128,512]{1,0:T(8,128)(2,1)S(1)}, u32[]{:S(2)}, u32[]{:S(2)}) %collective-permute-start.6) | collective-permute-done | bytes 131104 | tf_op jit(solution)/shard_map/ppermute | solution.py:14
  112.6 6.5 %collective-permute-start.7 = (bf16[128,512]{1,0:T(8,128)(2,1)S(1)}, bf16[128,512]{1,0:T(8,128)(2,1)S(1)}, u32[]{:S(2)}, u32[]{:S(2)}) collective-permute-start(bf16[128,512]{1,0:T(8,128)(2,1)S(1)} %collective-permute-done.6), channel_id=1, source_target_pairs={{0,1},{1,2},{2,3},{3,0},{4,5},{5,6},{6,7},{7,4},{8,9},{9,10},{10,1... | collective-permute-start | bytes 393224 | tf_op jit(solution)/shard_map/ppermute | solution.py:14
  119.1 3.8 %collective-permute-done.7 = bf16[128,512]{1,0:T(8,128)(2,1)S(1)} collective-permute-done((bf16[128,512]{1,0:T(8,128)(2,1)S(1)}, bf16[128,512]{1,0:T(8,128)(2,1)S(1)}, u32[]{:S(2)}, u32[]{:S(2)}) %collective-permute-start.7) | collective-permute-done | bytes 131104 | tf_op jit(solution)/shard_map/ppermute | solution.py:14
  122.9 2.5 %collective-permute-start.8 = (bf16[128,512]{1,0:T(8,128)(2,1)S(1)}, bf16[128,512]{1,0:T(8,128)(2,1)S(1)}, u32[]{:S(2)}, u32[]{:S(2)}) collective-permute-start(bf16[128,512]{1,0:T(8,128)(2,1)S(1)} %collective-permute-done.7), channel_id=1, source_target_pairs={{0,1},{1,2},{2,3},{3,0},{4,5},{5,6},{6,7},{7,4},{8,9},{9,10},{10,1... | collective-permute-start | bytes 393224 | tf_op jit(solution)/shard_map/ppermute | solution.py:14
  125.4 4.3 %collective-permute-done.8 = bf16[128,512]{1,0:T(8,128)(2,1)S(1)} collective-permute-done((bf16[128,512]{1,0:T(8,128)(2,1)S(1)}, bf16[128,512]{1,0:T(8,128)(2,1)S(1)}, u32[]{:S(2)}, u32[]{:S(2)}) %collective-permute-start.8) | collective-permute-done | bytes 131104 | tf_op jit(solution)/shard_map/ppermute | solution.py:14
  129.9 5.4 %gather_fusion.2 = bf16[1536,512]{1,0:T(8,128)(2,1)} fusion(bf16[512,512]{1,0:T(8,128)(2,1)S(1)} %constant_dynamic-slice_fusion, s32[2048]{0:T(1024)S(1)} %get-tuple-element.6), kind=kCustom, calls=%fused_computation.2 | custom fusion | bytes 3151872 | tf_op jit(solution)/shard_map/gather | solution.py:79
  135.3 3.7 %all-to-all-start.2 = ((bf16[4,384,128]{2,1,0:T(8,128)(2,1)}), bf16[4,384,128]{2,1,0:T(8,128)(2,1)S(1)}, u32[]{:S(2)}, u32[]{:S(2)}) async-start(bf16[4,384,128]{2,1,0:T(8,128)(2,1)} %bitcast.51), calls=%async_computation.2 | async-start | bytes 786432 | tf_op jit(solution)/shard_map/all_to_all | solution.py:73
  139.1 6.2 %fusion.6 = f32[4,384,1024]{2,1,0:T(8,128)} fusion(bf16[4,384,512]{2,1,0:T(8,128)(2,1)} %bitcast.40, bf16[1,1152,1024]{2,1,0:T(8,128)(2,1)} %param.15), kind=kOutput, calls=%fused_computation.16 | convolution fusion | flops 1610612736 | bytes 8912896 | tf_op jit(solution)/shard_map/ock,kh->och/dot_general | solution.py:78
  145.2 5.6 %fusion.8 = f32[4,384,1024]{2,1,0:T(8,128)} fusion(bf16[4,384,512]{2,1,0:T(8,128)(2,1)S(1)} %all-to-all-done.1, bf16[1,1152,1024]{2,1,0:T(8,128)(2,1)} %param.15), kind=kOutput, calls=%fused_computation.18 | convolution fusion | flops 1610612736 | bytes 8912896 | tf_op jit(solution)/shard_map/ock,kh->och/dot_general | solution.py:77
  150.9 8.0 %fusion.3 = bf16[4,384,512]{2,1,0:T(8,128)(2,1)S(1)} fusion(f32[4,384,1024]{2,1,0:T(8,128)} %fusion.8, f32[4,384,1024]{2,1,0:T(8,128)} %fusion.6, bf16[4,384,128]{2,1,0:T(8,128)(2,1)S(1)} %all-to-all-done.2, bf16[1,1024,512]{2,1,0:T(8,128)(2,1)S(1)} %copy-done, bf16[1,1152,1024]{2,1,0:T(8,128)(2,1)} %param.15), kind=kOutput, calls=%fused_computation.12 | convolution fusion | flops 2025062400 | bytes 15859712 | tf_op jit(solution)/shard_map/och,hd->ocd/dot_general | solution.py:83
  159.3 25.2 %all_to_all.24 = f32[4,128,512]{2,1,0:T(8,128)S(1)} all-to-all(f32[4,128,512]{2,1,0:T(8,128)S(1)} %fusion.12), channel_id=1, replica_groups=mesh['gx'=2,'gy'=4,'gz'=4] {'gz'}, dimensions={0} | all-to-all | bytes 2097152 | tf_op jit(solution)/shard_map/all_to_all | solution.py:91
  189.4 7.9 %collective-permute-done.12 = bf16[3,1,1,96,512]{4,3,2,1,0:T(8,128)(2,1)S(1)} collective-permute-done((bf16[3,1,1,96,512]{4,3,2,1,0:T(8,128)(2,1)S(1)}, bf16[3,1,1,96,512]{4,3,2,1,0:T(8,128)(2,1)S(1)}, u32[]{:S(2)}, u32[]{:S(2)}) %collective-permute-start.12) | collective-permute-done | bytes 294944 | tf_op jit(solution)/shard_map/ppermute | solution.py:34
  197.3 5.7 %collective-permute-done.11 = bf16[3,1,1,96,512]{4,3,2,1,0:T(8,128)(2,1)S(1)} collective-permute-done((bf16[3,1,1,96,512]{4,3,2,1,0:T(8,128)(2,1)S(1)}, bf16[3,1,1,96,512]{4,3,2,1,0:T(8,128)(2,1)S(1)}, u32[]{:S(2)}, u32[]{:S(2)}) %collective-permute-start.11) | collective-permute-done | bytes 294944 | tf_op jit(solution)/shard_map/ppermute | solution.py:33
  205.1 38.0 %collective-permute-done.14 = bf16[3,3,1,96,512]{4,3,2,1,0:T(8,128)(2,1)S(1)} collective-permute-done((bf16[3,3,1,96,512]{4,3,2,1,0:T(8,128)(2,1)S(1)}, bf16[3,3,1,96,512]{4,3,2,1,0:T(8,128)(2,1)S(1)}, u32[]{:S(2)}, u32[]{:S(2)}) %collective-permute-start.14) | collective-permute-done | bytes 884768 | tf_op jit(solution)/shard_map/ppermute | solution.py:34
  (74 shorter events, 17.6 us)
Async XLA Ops:
  0.6 150.3 %copy-start = (bf16[1,1024,512]{2,1,0:T(8,128)(2,1)S(1)}, bf16[1,1024,512]{2,1,0:T(8,128)(2,1)}, u32[]{:S(2)}) copy-start(bf16[1,1024,512]{2,1,0:T(8,128)(2,1)} %param.16) | copy-start | bytes 3145732
  0.6 25.9 %copy-start.8 = (s32[4]{0:T(128)S(1)}, s32[4]{0:T(128)}, u32[]{:S(2)}) copy-start(s32[4]{0:T(128)} %param.13) | copy-start | bytes 52
  0.7 25.9 %copy-start.6 = (s32[4,384]{1,0:T(4,128)S(1)}, s32[4,384]{1,0:T(4,128)}, u32[]{:S(2)}) copy-start(s32[4,384]{1,0:T(4,128)} %param.12) | copy-start | bytes 18436
  0.7 31.7 %copy-start.7 = (s32[4,384]{1,0:T(4,128)S(1)}, s32[4,384]{1,0:T(4,128)}, u32[]{:S(2)}) copy-start(s32[4,384]{1,0:T(4,128)} %param.11) | copy-start | bytes 18436
  3.1 1.5 collective-permute-start.1
  3.7 1.3 collective-permute-start
  5.0 11.0 %collective-permute-start.3 = (bf16[3,1,1,96,512]{4,3,2,1,0:T(8,128)(2,1)S(1)}, bf16[3,1,1,96,512]{4,3,2,1,0:T(8,128)(2,1)S(1)}, u32[]{:S(2)}, u32[]{:S(2)}) collective-permute-start(bf16[3,1,1,96,512]{4,3,2,1,0:T(8,128)(2,1)S(1)} %pad_maximum_fusion.7), channel_id=1, source_target_pairs={{4,0},{8,4},{12,8},{0,12},{5,1},{9,5},{13,9},{1,13},{6,2},{10,6},{... | collective-permute-start | bytes 884744 | tf_op jit(solution)/shard_map/ppermute | solution.py:34
  8.7 14.1 %collective-permute-start.2 = (bf16[3,1,1,96,512]{4,3,2,1,0:T(8,128)(2,1)S(1)}, bf16[3,1,1,96,512]{4,3,2,1,0:T(8,128)(2,1)S(1)}, u32[]{:S(2)}, u32[]{:S(2)}) collective-permute-start(bf16[3,1,1,96,512]{4,3,2,1,0:T(8,128)(2,1)S(1)} %pad_maximum_fusion.7), channel_id=1, source_target_pairs={{0,4},{4,8},{8,12},{12,0},{1,5},{5,9},{9,13},{13,1},{2,6},{6,10},{... | collective-permute-start | bytes 884744 | tf_op jit(solution)/shard_map/ppermute | solution.py:33
  22.9 42.4 %collective-permute-start.5 = (bf16[3,3,1,96,512]{4,3,2,1,0:T(8,128)(2,1)S(1)}, bf16[3,3,1,96,512]{4,3,2,1,0:T(8,128)(2,1)S(1)}, u32[]{:S(2)}, u32[]{:S(2)}) collective-permute-start(bf16[3,3,1,96,512]{4,3,2,1,0:T(8,128)(2,1)S(1)} %pad_maximum_fusion.5), channel_id=1, source_target_pairs={{1,0},{2,1},{3,2},{0,3},{5,4},{6,5},{7,6},{4,7},{9,8},{10,9},{11,1... | collective-permute-start | bytes 2654216 | tf_op jit(solution)/shard_map/ppermute | solution.py:34
  26.5 38.7 %collective-permute-start.4 = (bf16[3,3,1,96,512]{4,3,2,1,0:T(8,128)(2,1)S(1)}, bf16[3,3,1,96,512]{4,3,2,1,0:T(8,128)(2,1)}, u32[]{:S(2)}, u32[]{:S(2)}) collective-permute-start(bf16[3,3,1,96,512]{4,3,2,1,0:T(8,128)(2,1)S(1)} %pad_maximum_fusion.5), channel_id=1, source_target_pairs={{0,1},{1,2},{2,3},{3,0},{4,5},{5,6},{6,7},{7,4},{8,9},{9,10},{10,1... | collective-permute-start | bytes 2654216 | tf_op jit(solution)/shard_map/ppermute | solution.py:33
  27.2 37.9 %all-to-all-start = ((s32[4,1,384]{2,1,0:T(1,128)}), s32[4,1,384]{2,1,0:T(1,128)S(1)}, u32[]{:S(2)}, u32[]{:S(2)}) async-start(s32[4,1,384]{2,1,0:T(1,128)} %all_to_all.15), calls=%async_computation | async-start | bytes 12288 | tf_op jit(solution)/shard_map/all_to_all | solution.py:74
  77.1 58.2 %all-to-all-start.1 = ((bf16[4,384,512]{2,1,0:T(8,128)(2,1)}), bf16[4,384,512]{2,1,0:T(8,128)(2,1)S(1)}, u32[]{:S(2)}, u32[]{:S(2)}) async-start(bf16[4,384,512]{2,1,0:T(8,128)(2,1)} %bitcast.3), calls=%async_computation.1 | async-start | bytes 3145728 | tf_op jit(solution)/shard_map/all_to_all | solution.py:72
  81.7 30.9 %collective-permute-start.6 = (bf16[128,512]{1,0:T(8,128)(2,1)S(1)}, bf16[128,512]{1,0:T(8,128)(2,1)S(1)}, u32[]{:S(2)}, u32[]{:S(2)}) collective-permute-start(bf16[128,512]{1,0:T(8,128)(2,1)S(1)} %copy-done.1), channel_id=1, source_target_pairs={{0,1},{1,2},{2,3},{3,0},{4,5},{5,6},{6,7},{7,4},{8,9},{9,10},{10,1... | collective-permute-start | bytes 393224 | tf_op jit(solution)/shard_map/ppermute | solution.py:14
  112.6 10.3 %collective-permute-start.7 = (bf16[128,512]{1,0:T(8,128)(2,1)S(1)}, bf16[128,512]{1,0:T(8,128)(2,1)S(1)}, u32[]{:S(2)}, u32[]{:S(2)}) collective-permute-start(bf16[128,512]{1,0:T(8,128)(2,1)S(1)} %collective-permute-done.6), channel_id=1, source_target_pairs={{0,1},{1,2},{2,3},{3,0},{4,5},{5,6},{6,7},{7,4},{8,9},{9,10},{10,1... | collective-permute-start | bytes 393224 | tf_op jit(solution)/shard_map/ppermute | solution.py:14
  122.9 6.8 %collective-permute-start.8 = (bf16[128,512]{1,0:T(8,128)(2,1)S(1)}, bf16[128,512]{1,0:T(8,128)(2,1)S(1)}, u32[]{:S(2)}, u32[]{:S(2)}) collective-permute-start(bf16[128,512]{1,0:T(8,128)(2,1)S(1)} %collective-permute-done.7), channel_id=1, source_target_pairs={{0,1},{1,2},{2,3},{3,0},{4,5},{5,6},{6,7},{7,4},{8,9},{9,10},{10,1... | collective-permute-start | bytes 393224 | tf_op jit(solution)/shard_map/ppermute | solution.py:14
  135.3 15.5 %all-to-all-start.2 = ((bf16[4,384,128]{2,1,0:T(8,128)(2,1)}), bf16[4,384,128]{2,1,0:T(8,128)(2,1)S(1)}, u32[]{:S(2)}, u32[]{:S(2)}) async-start(bf16[4,384,128]{2,1,0:T(8,128)(2,1)} %bitcast.51), calls=%async_computation.2 | async-start | bytes 786432 | tf_op jit(solution)/shard_map/all_to_all | solution.py:73
  158.9 25.8 %copy-start.5 = (bf16[512,512]{1,0:T(8,128)(2,1)S(1)}, bf16[512,512]{1,0:T(8,128)(2,1)}, u32[]{:S(2)}) copy-start(bf16[512,512]{1,0:T(8,128)(2,1)} %param.17) | copy-start | bytes 1572868
  185.0 58.5 %copy-start.2 = (bf16[128,512]{1,0:T(8,128)(2,1)}, bf16[128,512]{1,0:T(8,128)(2,1)S(1)}, u32[]{:S(2)}) copy-start(bf16[128,512]{1,0:T(8,128)(2,1)S(1)} %fusion.4) | copy-start | bytes 393220
  185.8 1.4 collective-permute-start.10
  185.9 1.4 collective-permute-start.9
  187.3 9.9 %collective-permute-start.12 = (bf16[3,1,1,96,512]{4,3,2,1,0:T(8,128)(2,1)S(1)}, bf16[3,1,1,96,512]{4,3,2,1,0:T(8,128)(2,1)S(1)}, u32[]{:S(2)}, u32[]{:S(2)}) collective-permute-start(bf16[3,1,1,96,512]{4,3,2,1,0:T(8,128)(2,1)S(1)} %pad_maximum_fusion.8), channel_id=1, source_target_pairs={{4,0},{8,4},{12,8},{0,12},{5,1},{9,5},{13,9},{1,13},{6,2},{10,6},{... | collective-permute-start | bytes 884744 | tf_op jit(solution)/shard_map/ppermute | solution.py:34
  188.8 14.1 %collective-permute-start.11 = (bf16[3,1,1,96,512]{4,3,2,1,0:T(8,128)(2,1)S(1)}, bf16[3,1,1,96,512]{4,3,2,1,0:T(8,128)(2,1)S(1)}, u32[]{:S(2)}, u32[]{:S(2)}) collective-permute-start(bf16[3,1,1,96,512]{4,3,2,1,0:T(8,128)(2,1)S(1)} %pad_maximum_fusion.8), channel_id=1, source_target_pairs={{0,4},{4,8},{8,12},{12,0},{1,5},{5,9},{9,13},{13,1},{2,6},{6,10},{... | collective-permute-start | bytes 884744 | tf_op jit(solution)/shard_map/ppermute | solution.py:33
  203.0 40.1 %collective-permute-start.14 = (bf16[3,3,1,96,512]{4,3,2,1,0:T(8,128)(2,1)S(1)}, bf16[3,3,1,96,512]{4,3,2,1,0:T(8,128)(2,1)S(1)}, u32[]{:S(2)}, u32[]{:S(2)}) collective-permute-start(bf16[3,3,1,96,512]{4,3,2,1,0:T(8,128)(2,1)S(1)} %pad_maximum_fusion.6), channel_id=1, source_target_pairs={{1,0},{2,1},{3,2},{0,3},{5,4},{6,5},{7,6},{4,7},{9,8},{10,9},{11,1... | collective-permute-start | bytes 2654216 | tf_op jit(solution)/shard_map/ppermute | solution.py:34
  204.6 38.6 %collective-permute-start.13 = (bf16[3,3,1,96,512]{4,3,2,1,0:T(8,128)(2,1)S(1)}, bf16[3,3,1,96,512]{4,3,2,1,0:T(8,128)(2,1)S(1)}, u32[]{:S(2)}, u32[]{:S(2)}) collective-permute-start(bf16[3,3,1,96,512]{4,3,2,1,0:T(8,128)(2,1)S(1)} %pad_maximum_fusion.6), channel_id=1, source_target_pairs={{0,1},{1,2},{2,3},{3,0},{4,5},{5,6},{6,7},{7,4},{8,9},{9,10},{10,1... | collective-permute-start | bytes 2654216 | tf_op jit(solution)/shard_map/ppermute | solution.py:33
  (3 other events, 44.4 us)
